TPU v7x, 256 devices: a whole 4x4x8 slice. The times are simulated.
256 devices in a mesh: section: 16 (over y, z_lo), dp: 8 (over z_hi, x), tensor: 2 (over core).
Axes of the slice: x: 4, y: 4, z: 8 (z_hi: 2, z_lo: 4; z = z_hi * 4 + z_lo), core: 2. Of those that a mesh axis runs over, the one named last changes fastest.
Arguments:
- context: bfloat16 [16, 16, 256, 2048], P('section', 'dp'), may hold values from -6 to 6
- queries: bfloat16 [16, 16, 64, 2048], P('section', 'dp'), may hold values from -6 to 6
- lengths: int32 [16, 16], P('section', 'dp'), may hold values from 32 to 256
- norm_gain: float32 [16, 2048], P('section'), may hold values from 0.1 to 1.9
- qkv_weight: bfloat16 [16, 2048, 3, 2048], P('section', 'dp', None, 'tensor')
- out_weight: bfloat16 [16, 2048, 2048], P('section', 'tensor', 'dp'), may hold values from -0.5 to 0.5
Outputs:
- next_context: bfloat16 [16, 16, 256, 2048], P('section', 'dp')
- next_queries: bfloat16 [16, 16, 64, 2048], P('section', 'dp')
All inputs are finite; a program needn't handle non-finite values.
Results may differ from a plain program's by a relative error of at most 0.014.
The roundings to bfloat16 on the way count: a program that leaves them out, or rounds other values in their place, can miss the bound.
Values may be sent and summed in bfloat16 or wider, within the bound.
No kernel may reach another device: no remote copies, remote signals or barrier semaphores. Data moves between devices by JAX's collectives and lax.ppermute only.
A program may use at most 128 MiB of HBM per device.

v0:
```python
import math
import jax
import jax.numpy as jnp
from jax import lax
from jax.sharding import PartitionSpec as P

HEAD = 128


def from_behind(array, axis, by):
    count = lax.axis_size(axis)
    return lax.ppermute(array, axis, [(i, (i + by) % count) for i in range(count)])


def attend(projected, valid_len, first_row, row_count, memory_rows):
    query_part = projected[:, first_row : first_row + row_count, 0]
    key_part = projected[:, :memory_rows, 1]
    value_part = projected[:, :memory_rows, 2]
    scores = jnp.einsum(
        "brhd,bjhd->bhrj", query_part, key_part, preferred_element_type=jnp.float32
    ) * (1.0 / math.sqrt(HEAD))
    key_index = jnp.arange(memory_rows, dtype=jnp.int32)
    valid = key_index[None, None, None, :] < valid_len[:, None, None, None]
    scores = jnp.where(valid, scores, -1e30)
    top_score = jnp.max(scores, axis=-1, keepdims=True)
    expo = jnp.exp(scores - top_score)
    probs = (expo / jnp.sum(expo, axis=-1, keepdims=True)).astype(jnp.bfloat16)
    mixed = jnp.einsum(
        "bhrj,bjhd->brhd", probs, value_part, preferred_element_type=jnp.float32
    ).astype(jnp.bfloat16)
    return mixed


def per_device(context, queries, lengths, norm_gain, qkv_weight, out_weight):
    context_rows = context[0]
    query_rows = queries[0]
    stream_rows = jnp.concatenate([context_rows, query_rows], axis=1)
    scene_count = stream_rows.shape[0]
    row_total = stream_rows.shape[1]
    model_width = stream_rows.shape[2]
    memory_rows = context.shape[2]
    local_width = qkv_weight.shape[3]
    head_count = local_width // HEAD
    encoder_flag = lax.axis_index("section") < lax.axis_size("section") // 2
    widened = stream_rows.astype(jnp.float32)
    mean_square = jnp.mean(widened * widened, axis=-1, keepdims=True)
    normed = (widened * lax.rsqrt(mean_square + 1e-06) * norm_gain[0]).astype(jnp.bfloat16)
    flat_rows = normed.reshape(scene_count * row_total, model_width)
    weight_rows = lax.all_gather(qkv_weight, "dp", axis=1, tiled=True)
    row_count = weight_rows.shape[1]
    projected = jnp.dot(
        flat_rows,
        weight_rows[0].reshape(row_count, 3 * local_width),
        preferred_element_type=jnp.float32,
    )
    projected = projected.astype(jnp.bfloat16).reshape(scene_count, row_total, 3, head_count, HEAD)
    mixed = attend(projected, lengths[0], 0, row_total, memory_rows)
    row_index = jnp.arange(row_total, dtype=jnp.int32)
    keep_rows = jnp.where(encoder_flag, row_index < memory_rows, row_index >= memory_rows)
    mixed = mixed * keep_rows[None, :, None, None].astype(jnp.bfloat16)
    mixed_flat = mixed.reshape(scene_count * row_total, local_width)
    update = jnp.dot(
        mixed_flat,
        lax.all_gather(out_weight, "dp", axis=2, tiled=True)[0],
        preferred_element_type=jnp.float32,
    )
    update = update.reshape(scene_count, row_total, model_width)
    head_total = lax.psum(update.astype(jnp.bfloat16), "tensor").astype(jnp.float32)
    fresh = (widened + head_total).astype(jnp.bfloat16)
    context_new = fresh[:, :memory_rows]
    query_new = fresh[:, memory_rows:]
    passed = from_behind((context_new, query_new), "section", 1)
    return (passed[0][None], passed[1][None])


def solution(mesh):
    return jax.shard_map(
        per_device,
        mesh=mesh,
        in_specs=(
            P("section", "dp", None, None),
            P("section", "dp", None, None),
            P("section", "dp"),
            P("section", None),
            P("section", "dp", None, "tensor"),
            P("section", "tensor", "dp"),
        ),
        out_specs=(P("section", "dp", None, None), P("section", "dp", None, None)),
        check_vma=False,
    )
```

profile of v0, /device:TPU:1, one launch (start us, length us, event | category | flops | bytes accessed | tf_op | source)
XLA Modules:
  0.0 489.0 jit_solution(638077608019087004)
XLA Ops:
  7.3 2.7 copy.11
  10.0 0.0 all-gather.5.cloned.1.call-start
  10.1 0.7 all-gather.5.cloned.1.call-update
  10.8 0.6 fusion.1
  11.4 0.1 iota_compare_fusion.2
  11.5 2.2 fusion.3
  13.7 254.5 %all-gather.3.cloned.1.call-done = bf16[1,2048,3,1024]{1,3,2,0:T(8,128)(2,1)} async-done(((bf16[1,256,3,1024]{1,3,2,0:T(8,128)(2,1)}), bf16[1,2048,3,1024]{1,3,2,0:T(8,128)(2,1)}) %all-gather.3.cloned.1.call-update) | async-done | bytes 12582928 | tf_op jit(solution)/shard_map/all_gather | solution.py:49
  268.2 12.1 %fusion.15 = bf16[80,8,24,128]{3,1,2,0:T(8,128)(2,1)S(1)} fusion(bf16[640,2048]{1,0:T(8,128)(2,1)} %bitcast.43, bf16[2048,3072]{0,1:T(8,128)(2,1)} %bitcast.47), kind=kOutput, calls=%fused_computation.21 | convolution fusion | flops 8055029760 | bytes 19136512 | tf_op jit(solution)/shard_map/dot_general | solution.py:51
  280.3 1.1 copy.20
  281.5 0.1 slice.20
  281.5 0.4 fusion.24
  281.9 0.9 fusion.19
  282.8 2.4 fusion.25
  285.2 2.0 multiply_bitcast_fusion
  287.2 90.6 %all-gather.5.cloned.1.call-done = bf16[1,1024,2048]{2,1,0:T(8,128)(2,1)} async-done(((bf16[1,1024,256]{2,1,0:T(8,128)(2,1)}), bf16[1,1024,2048]{2,1,0:T(8,128)(2,1)}) %all-gather.5.cloned.1.call-update) | async-done | bytes 4194320 | tf_op jit(solution)/shard_map/all_gather | solution.py:64
  377.7 7.0 %fusion.8 = bf16[2,320,2048]{2,1,0:T(8,128)(2,1)} fusion(bf16[1,1024,2048]{2,1,0:T(8,128)(2,1)} %all-gather.5.cloned.1.call-done, bf16[2,8,40,8,128]{4,3,2,1,0:T(8,128)(2,1)} %multiply_bitcast_fusion), kind=kOutput, calls=%fused_computation.15 | convolution fusion | flops 2685665280 | bytes 8126464 | tf_op jit(solution)/shard_map/dot_general | solution.py:62
  384.7 30.4 %all-reduce.2.cloned.1.call-done = bf16[2,320,2048]{2,1,0:T(8,128)(2,1)} async-done(((bf16[2,320,2048]{2,1,0:T(8,128)(2,1)}), bf16[2,320,2048]{2,1,0:T(8,128)(2,1)}) %all-reduce.2.cloned.1.call-update) | async-done | bytes 2621456 | tf_op jit(solution)/shard_map/psum | solution.py:68
  415.2 2.8 fusion.4
  418.0 0.1 slice.23
  418.1 1.1 collective-permute-start
  419.3 1.4 collective-permute-start.1
  420.6 59.8 %collective-permute-done.1 = bf16[2,64,2048]{2,1,0:T(8,128)(2,1)S(1)} collective-permute-done((bf16[2,64,2048]{2,1,0:T(8,128)(2,1)S(1)}, bf16[2,64,2048]{2,1,0:T(8,128)(2,1)S(1)}, u32[]{:S(2)}, u32[]{:S(2)}) %collective-permute-start.1) | collective-permute-done | bytes 524320 | tf_op jit(solution)/shard_map/ppermute | solution.py:12
  480.4 1.3 copy.34
  481.7 0.8 copy.35
  (16 shorter events, 0.2 us)
Async XLA Ops:
  7.2 3.7 copy-start
  7.2 3.7 copy-start.1
  7.2 4.3 copy-start.3
  7.2 4.3 copy-start.2
  7.2 261.0 %all-gather.3.cloned.1.call-start = ((), (), s32[]{:S(2)}) async-start(), calls=%async_computation | async-start | bytes 14155776 | tf_op jit(solution)/shard_map/all_gather | solution.py:49
  10.0 367.7 %all-gather.5.cloned.1.call-start = ((), (), s32[]{:S(2)}) async-start(), calls=%async_computation.1 | async-start | bytes 4718592 | tf_op jit(solution)/shard_map/all_gather | solution.py:64
  10.8 404.4 %all-reduce.2.cloned.1.call-start = ((), (), s32[]{:S(2)}) async-start(), calls=%async_computation.2 | async-start | bytes 5242880 | tf_op jit(solution)/shard_map/psum | solution.py:68
  418.1 62.2 %collective-permute-start = (bf16[2,256,2048]{2,1,0:T(8,128)(2,1)S(1)}, bf16[2,256,2048]{2,1,0:T(8,128)(2,1)S(1)}, u32[]{:S(2)}, u32[]{:S(2)}) collective-permute-start(bf16[2,256,2048]{2,1,0:T(8,128)(2,1)S(1)} %slice.23), channel_id=1, source_target_pairs={{0,16},{16,32},{32,48},{48,64},{64,80},{80,96},{96,112},{112,128},... | collective-permute-start | bytes 6291464 | tf_op jit(solution)/shard_map/ppermute | solution.py:12
  419.3 61.1 %collective-permute-start.1 = (bf16[2,64,2048]{2,1,0:T(8,128)(2,1)S(1)}, bf16[2,64,2048]{2,1,0:T(8,128)(2,1)S(1)}, u32[]{:S(2)}, u32[]{:S(2)}) collective-permute-start(bf16[2,64,2048]{2,1,0:T(8,128)(2,1)S(1)} %slice.24), channel_id=1, source_target_pairs={{0,16},{16,32},{32,48},{48,64},{64,80},{80,96},{96,112},{112,128},... | collective-permute-start | bytes 1572872 | tf_op jit(solution)/shard_map/ppermute | solution.py:12
Sparse Core Ops, SparseCore 0:
  11.1 257.0 all-gather.2
  270.7 107.0 all-gather.4
  384.9 30.2 all-reduce.1
where the time goes:
time: 489 us
  waiting for transfers between devices  436 us (89%)
  matrix products  21.9 us (4%)
  between operations  13.9 us (3%)
  other arithmetic  8.03 us (2%)
  local copies, waits for them, and re-layouts  6.61 us (1%)
    all_gather x1, waiting for transfers between devices, per_device(): weight_rows = lax.all_gather(qkv_weight, 'dp', axis=1, tiled=True)  255 us
    all_gather x1, waiting for transfers between devices, per_device(): lax.all_gather(out_weight, 'dp', axis=2, tiled=True)[0]  90.6 us
    ppermute x2, waiting for transfers between devices, from_behind(): lax.ppermute(array, axis, [(i, (i + by) % count) for i in range(count)])  59.8 us
    psum x1, waiting for transfers between devices, per_device(): lax.psum(update.astype(jnp.bfloat16), 'tensor').astype(jnp.float32)  30.4 us
    dot_general x1, matrix products, per_device(): jnp.dot(flat_rows, weight_rows[0].reshape(row_count, 3 * local_width), pr...  12.1 us
  transfers between devices with their start and end apart: 5, of which 4 were waited for; matrix products, arithmetic and copies ran while one was open for 4% of the time, Pallas kernels for 0%

commit v1 on v0

--- a/solution.py
+++ b/solution.py
@@ -61,7 +61,9 @@
     mixed_flat = mixed.reshape(scene_count * row_total, local_width)
     update = jnp.dot(
         mixed_flat,
-        lax.all_gather(out_weight, "dp", axis=2, tiled=True)[0],
+        jnp.concatenate(
+            lax.all_to_all(jnp.stack([out_weight] * lax.axis_size("dp")), "dp", 0, 0), axis=2
+        )[0],
         preferred_element_type=jnp.float32,
     )
     update = update.reshape(scene_count, row_total, model_width)

time: 489 us -> 468 us (0.957)
  waiting for transfers between devices: 436 us -> 389 us
  local copies, waits for them, and re-layouts: 6.61 us -> 23.6 us
  starting transfers between devices: 2.56 us -> 14.3 us
    all_to_all x0 -> x1, waiting for transfers between devices: none -> 92.1 us  [per_device(): lax.all_to_all(jnp.stack([out_weight] * lax.axis_size('dp')), 'dp', 0, 0)]
    all_gather x1 -> x0, waiting for transfers between devices: 90.6 us -> none  [per_device(): lax.all_gather(out_weight, 'dp', axis=2, tiled=True)[0]]
    all_gather x1, waiting for transfers between devices: 255 us -> 207 us  [per_device(): weight_rows = lax.all_gather(qkv_weight, 'dp', axis=1, tiled=True)]
    all_to_all x0 -> x1, starting transfers between devices: none -> 11.8 us  [per_device(): lax.all_to_all(jnp.stack([out_weight] * lax.axis_size('dp')), 'dp', 0, 0)]
    another operation x0 -> x2, local copies, waits for them, and re-layouts: none -> 9.62 us  [the longest x1 7.41 us: per_device(): jnp.concatenate(lax.all_to_all(jnp.stack([out_weight] * lax.axis_size('dp...]
    reshape x0 -> x1, local copies, waits for them, and re-layouts: none -> 6.5 us  [per_device(): jnp.concatenate(lax.all_to_all(jnp.stack([out_weight] * lax.axis_size('dp...]
where the time goes in v1:
time: 468 us; the launch traced here: 467 us
  waiting for transfers between devices  389 us (83%)
  local copies, waits for them, and re-layouts  23.6 us (5%)
  matrix products  18.4 us (4%)
  starting transfers between devices  14.3 us (3%)
  between operations  14.2 us (3%)
  other arithmetic  8.04 us (2%)
    all_gather x1, waiting for transfers between devices, per_device(): weight_rows = lax.all_gather(qkv_weight, 'dp', axis=1, tiled=True)  207 us
    all_to_all x1, waiting for transfers between devices, per_device(): lax.all_to_all(jnp.stack([out_weight] * lax.axis_size('dp')), 'dp', 0, 0)  92.1 us
    ppermute x2, waiting for transfers between devices, from_behind(): lax.ppermute(array, axis, [(i, (i + by) % count) for i in range(count)])  59.8 us
    psum x1, waiting for transfers between devices, per_device(): lax.psum(update.astype(jnp.bfloat16), 'tensor').astype(jnp.float32)  30.3 us
    dot_general x1, matrix products, per_device(): jnp.dot(flat_rows, weight_rows[0].reshape(row_count, 3 * local_width), pr...  12.1 us
    all_to_all x1, starting transfers between devices, per_device(): lax.all_to_all(jnp.stack([out_weight] * lax.axis_size('dp')), 'dp', 0, 0)  11.8 us
  transfers between devices with their start and end apart: 5, of which 4 were waited for; matrix products, arithmetic and copies ran while one was open for 4% of the time, Pallas kernels for 0%

profile of v1, /device:TPU:1, one launch (start us, length us, event | category | flops | bytes accessed | tf_op | source)
XLA Modules:
  0.0 467.4 jit_solution(12416733342367653692)
XLA Ops:
  7.2 2.6 copy.16
  9.9 2.2 stack.2
  12.1 11.8 %all-to-all-start = ((bf16[8,1,1024,256]{3,2,1,0:T(8,128)(2,1)}), bf16[8,1,1024,256]{3,2,1,0:T(8,128)(2,1)}, u32[]{:S(2)}, u32[]{:S(2)}) async-start(bf16[8,1,1024,256]{3,2,1,0:T(8,128)(2,1)} %stack.2), calls=%async_computation | async-start | bytes 8388608 | tf_op jit(solution)/shard_map/all_to_all | solution.py:65
  23.9 0.6 fusion.1
  24.6 2.2 fusion.3
  26.8 92.1 %all-to-all-done = bf16[8,1,1024,256]{3,2,1,0:T(8,128)(2,1)} async-done(((bf16[8,1,1024,256]{3,2,1,0:T(8,128)(2,1)}), bf16[8,1,1024,256]{3,2,1,0:T(8,128)(2,1)}, u32[]{:S(2)}, u32[]{:S(2)}) %all-to-all-start) | async-done | bytes 4194336 | tf_op jit(solution)/shard_map/all_to_all | solution.py:65
  118.9 6.5 %copy.21 = bf16[1,1024,8,256]{3,2,1,0:T(8,128)(2,1)} copy(bf16[1,1024,8,256]{3,1,0,2:T(8,128)(2,1)} %bitcast.11) | data formatting | bytes 8388608 | tf_op jit(solution)/shard_map/reshape | solution.py:64
  125.4 7.4 %reshape.117 = bf16[1024,2048,1]{1,0,2:T(8,128)(2,1)} reshape(bf16[1,1024,8,256]{3,2,1,0:T(8,128)(2,1)} %copy.21) | data formatting | bytes 8388608 | tf_op jit(solution)/shard_map/squeeze;reshape | solution.py:64
  132.8 206.7 %all-gather.2.cloned.1.call-done = bf16[1,2048,3,1024]{1,3,2,0:T(8,128)(2,1)} async-done(((bf16[1,256,3,1024]{1,3,2,0:T(8,128)(2,1)}), bf16[1,2048,3,1024]{1,3,2,0:T(8,128)(2,1)}) %all-gather.2.cloned.1.call-update) | async-done | bytes 12582928 | tf_op jit(solution)/shard_map/all_gather | solution.py:49
  339.6 12.1 %fusion.10 = bf16[80,8,24,128]{3,1,2,0:T(8,128)(2,1)S(1)} fusion(bf16[640,2048]{1,0:T(8,128)(2,1)} %bitcast.42, bf16[2048,3072]{0,1:T(8,128)(2,1)} %bitcast.47), kind=kOutput, calls=%fused_computation.19 | convolution fusion | flops 8055029760 | bytes 19136512 | tf_op jit(solution)/shard_map/dot_general | solution.py:51
  351.7 1.1 copy.26
  352.8 0.4 fusion.19
  353.3 0.9 fusion.14
  354.2 2.4 fusion.20
  356.6 1.2 multiply_bitcast_fusion
  357.7 1.0 copy-done.2
  358.7 4.2 convolution_convert_fusion.1
  363.0 30.3 %all-reduce.2.cloned.1.call-done = bf16[2,320,2048]{2,1,0:T(8,128)(2,1)} async-done(((bf16[2,320,2048]{2,1,0:T(8,128)(2,1)}), bf16[2,320,2048]{2,1,0:T(8,128)(2,1)}) %all-reduce.2.cloned.1.call-update) | async-done | bytes 2621456 | tf_op jit(solution)/shard_map/psum | solution.py:70
  393.3 2.8 fusion.4
  396.2 1.1 collective-permute-start
  397.4 1.4 collective-permute-start.1
  398.7 59.8 %collective-permute-done.1 = bf16[2,64,2048]{2,1,0:T(8,128)(2,1)S(1)} collective-permute-done((bf16[2,64,2048]{2,1,0:T(8,128)(2,1)S(1)}, bf16[2,64,2048]{2,1,0:T(8,128)(2,1)S(1)}, u32[]{:S(2)}, u32[]{:S(2)}) %collective-permute-start.1) | collective-permute-done | bytes 524320 | tf_op jit(solution)/shard_map/ppermute | solution.py:12
  458.5 1.3 copy.40
  459.8 0.8 copy.41
  (22 shorter events, 0.5 us)
Async XLA Ops:
  7.2 2.7 copy-start.3
  7.2 332.4 %all-gather.2.cloned.1.call-start = ((), (), s32[]{:S(2)}) async-start(), calls=%async_computation.1 | async-start | bytes 14155776 | tf_op jit(solution)/shard_map/all_gather | solution.py:49
  12.1 11.8 %copy-start = (bf16[1,2,256,2048]{3,2,1,0:T(8,128)(2,1)S(1)}, bf16[1,2,256,2048]{3,2,1,0:T(8,128)(2,1)}, u32[]{:S(2)}) copy-start(bf16[1,2,256,2048]{3,2,1,0:T(8,128)(2,1)} %param.6) | copy-start | bytes 6291460
  12.1 11.8 %copy-start.1 = (bf16[1,2,64,2048]{3,2,1,0:T(8,128)(2,1)S(1)}, bf16[1,2,64,2048]{3,2,1,0:T(8,128)(2,1)}, u32[]{:S(2)}) copy-start(bf16[1,2,64,2048]{3,2,1,0:T(8,128)(2,1)} %param.7) | copy-start | bytes 1572868
  12.1 12.4 %copy-start.5 = (s32[1,2]{1,0:T(1,128)S(1)}, s32[1,2]{1,0:T(1,128)}, u32[]{:S(2)}) copy-start(s32[1,2]{1,0:T(1,128)} %param.8) | copy-start | bytes 28
  12.1 12.5 %copy-start.4 = (f32[1,2048]{1,0:T(1,128)S(1)}, f32[1,2048]{1,0:T(1,128)}, u32[]{:S(2)}) copy-start(f32[1,2048]{1,0:T(1,128)} %param.9) | copy-start | bytes 24580
  12.1 106.8 %all-to-all-start = ((bf16[8,1,1024,256]{3,2,1,0:T(8,128)(2,1)}), bf16[8,1,1024,256]{3,2,1,0:T(8,128)(2,1)}, u32[]{:S(2)}, u32[]{:S(2)}) async-start(bf16[8,1,1024,256]{3,2,1,0:T(8,128)(2,1)} %stack.2), calls=%async_computation | async-start | bytes 8388608 | tf_op jit(solution)/shard_map/all_to_all | solution.py:65
  23.8 369.4 %all-reduce.2.cloned.1.call-start = ((), (), s32[]{:S(2)}) async-start(), calls=%async_computation.2 | async-start | bytes 5242880 | tf_op jit(solution)/shard_map/psum | solution.py:70
  356.5 2.2 copy-start.2
  396.2 62.2 %collective-permute-start = (bf16[2,256,2048]{2,1,0:T(8,128)(2,1)S(1)}, bf16[2,256,2048]{2,1,0:T(8,128)(2,1)S(1)}, u32[]{:S(2)}, u32[]{:S(2)}) collective-permute-start(bf16[2,256,2048]{2,1,0:T(8,128)(2,1)S(1)} %slice.23), channel_id=1, source_target_pairs={{0,16},{16,32},{32,48},{48,64},{64,80},{80,96},{96,112},{112,128},... | collective-permute-start | bytes 6291464 | tf_op jit(solution)/shard_map/ppermute | solution.py:12
  397.4 61.1 %collective-permute-start.1 = (bf16[2,64,2048]{2,1,0:T(8,128)(2,1)S(1)}, bf16[2,64,2048]{2,1,0:T(8,128)(2,1)S(1)}, u32[]{:S(2)}, u32[]{:S(2)}) collective-permute-start(bf16[2,64,2048]{2,1,0:T(8,128)(2,1)S(1)} %slice.24), channel_id=1, source_target_pairs={{0,16},{16,32},{32,48},{48,64},{64,80},{80,96},{96,112},{112,128},... | collective-permute-start | bytes 1572872 | tf_op jit(solution)/shard_map/ppermute | solution.py:12
Sparse Core Ops, SparseCore 0:
  11.1 328.4 all-gather.1
  363.1 30.1 all-reduce.1
